TPU v7x, 32 devices: a whole 2x2x4 slice. The times are simulated.
32 devices in a mesh: book: 2 (over y), seq: 4 (over x, core), sub: 4 (over z).
Axes of the slice: x: 2, y: 2, z: 4, core: 2. Of those that a mesh axis runs over, the one named last changes fastest.
Arguments:
- queries: bfloat16 [16384, 2048], P(('book', 'seq'), 'sub'), parts along dimension 0, may hold values from -4 to 1920
- keys: bfloat16 [16384, 2048], P(('book', 'seq'), 'sub'), parts along dimension 0, may hold values from -6 to 4
- values: bfloat16 [16384, 2048], P(('book', 'seq'), 'sub'), parts along dimension 0, may hold values from -6 to 6
- decay: float32 [8, 8], P('book', 'sub'), parts along dimension 0, may hold values from 0.05 to 1
- gate: float32 [8], P('sub'), may hold values from -0.5 to 3
- summary: bfloat16 [512, 2048], P(('book', 'seq')), parts along dimension 0, may hold values from -6 to 6
- wq_sum: bfloat16 [2048, 2048], P(None, 'sub'), may hold values from -0.25 to 0.25
- wo_sum: bfloat16 [2048, 2048], P('sub'), may hold values from -0.125 to 0.125
Outputs:
- attended: bfloat16 [16384, 2048], P(('book', 'seq'), 'sub'), parts along dimension 0
- summarized: bfloat16 [512, 2048], P(('book', 'seq')), parts along dimension 0
There are 2 independent parts, one for each index of `book`. A program takes and returns all parts, laid end to end along the dimension named above; an argument that names none is the same for every part. Nothing has to cross between parts.
All inputs are finite; a program needn't handle non-finite values.
Results may differ from a plain program's by a relative error of at most 0.019.
Values may be sent and summed in bfloat16 or wider, within the bound.
No kernel may reach another device: no remote copies, remote signals or barrier semaphores. Data moves between devices by JAX's collectives and lax.ppermute only.
A program may use at most 128 MiB of HBM per device.

v0:
```python
import jax
import jax.numpy as jnp
from jax import lax
from jax.sharding import PartitionSpec as P

SEG = 2048
STEPS = 4
top_precision = lax.Precision.HIGHEST


def carried_in(value, axis, join, neutral):
    count, mine = (lax.axis_size(axis), lax.axis_index(axis))
    pieces = jax.tree.map(lambda part: lax.all_gather(part, axis), value)
    so_far = jax.tree.map(
        lambda part, zero: jnp.full_like(part, 0) + jnp.asarray(zero, part.dtype), value, neutral
    )

    def step(position, so_far):
        longer = join(so_far, jax.tree.map(lambda part: part[position], pieces))
        return jax.tree.map(lambda new, old: jnp.where(position < mine, new, old), longer, so_far)

    return lax.fori_loop(0, count - 1, step, so_far)


def broadcast(x, axis, root):
    mine = lax.axis_index(axis) == root
    return lax.psum(jnp.where(mine, x, jnp.zeros_like(x)), axis)


def feature_map(inputs):
    return jax.nn.elu(inputs) + 1.0


def head_rms(inputs):
    return inputs * lax.rsqrt(jnp.mean(inputs * inputs, axis=-1, keepdims=True) + 1e-06)


def memory_read(lifted, memory, normalizer):
    numerator = jnp.einsum("qhd,hde->qhe", lifted, memory, precision=top_precision)
    denominator = jnp.einsum("qhd,hd->qh", lifted, normalizer, precision=top_precision) + 1.0
    return numerator / denominator[..., None]


def segment_attention(q_part, k_part, v_part):
    length = q_part.shape[0]
    block_rows = min(512, length)
    score_scale = q_part.shape[2] ** (-0.5)
    columns = jnp.arange(length)
    pieces = []
    for first_row in range(0, length, block_rows):
        scores = (
            jnp.einsum(
                "qhd,khd->hqk",
                q_part[first_row : first_row + block_rows],
                k_part,
                preferred_element_type=jnp.float32,
            )
            * score_scale
        )
        rows_here = first_row + jnp.arange(block_rows)
        scores = jnp.where(columns[None, None, :] <= rows_here[None, :, None], scores, -jnp.inf)
        weights = jax.nn.softmax(scores, axis=-1).astype(jnp.bfloat16)
        pieces.append(
            jnp.einsum("hqk,khd->qhd", weights, v_part, preferred_element_type=jnp.float32)
        )
    return jnp.concatenate(pieces, axis=0)


def on_device(queries, keys, values, decay, gate, summary, wq_sum, wo_sum):
    head_count = gate.shape[0]
    head_width = queries.shape[1] // head_count
    seg_count = queries.shape[0] // SEG
    position = lax.axis_index("seq")
    devices = lax.axis_size("seq")
    q_seg = queries.reshape(seg_count, SEG, head_count, head_width)
    k_seg = keys.reshape(seg_count, SEG, head_count, head_width)
    v_seg = values.reshape(seg_count, SEG, head_count, head_width)
    lifted_keys = feature_map(k_seg.astype(jnp.float32))
    updates = jnp.einsum(
        "jqhd,jqhe->jhde", lifted_keys, v_seg.astype(jnp.float32), precision=top_precision
    )
    key_sums = jnp.sum(lifted_keys, axis=1)
    local_decay = lax.dynamic_slice_in_dim(decay, position * seg_count, seg_count, 0)
    empty_memory = jnp.zeros((head_count, head_width, head_width), jnp.float32)
    empty_norm = jnp.zeros((head_count, head_width), jnp.float32)

    def accumulate(running, inputs_now):
        seg_decay, update, key_total = inputs_now
        return (
            (
                seg_decay[:, None, None] * running[0] + update,
                seg_decay[:, None] * running[1] + key_total,
            ),
            None,
        )

    (own_memory, own_norm), _ = lax.scan(
        accumulate, (empty_memory, empty_norm), (local_decay, updates, key_sums)
    )
    own_decay = jnp.prod(local_decay, axis=0)

    def combine(earlier, later):
        return (
            earlier[0] * later[0],
            later[0][:, None, None] * earlier[1] + later[1],
            later[0][:, None] * earlier[2] + later[2],
        )

    identity = (jnp.ones((head_count,), jnp.float32), empty_memory, empty_norm)
    _, prior_memory, prior_norm = carried_in(
        (own_decay, own_memory, own_norm), "seq", combine, identity
    )
    ending_memory = own_decay[:, None, None] * prior_memory + own_memory
    ending_norm = own_decay[:, None] * prior_norm + own_norm
    final_memory, final_norm = (
        broadcast(ending_memory, "seq", devices - 1),
        broadcast(ending_norm, "seq", devices - 1),
    )
    blend_weight = jax.nn.sigmoid(gate)[None, :, None]

    def one_segment(running, inputs_now):
        memory, normalizer = running
        q_part, k_part, v_part, seg_decay, update, key_total = inputs_now
        recalled = memory_read(feature_map(q_part.astype(jnp.float32)), memory, normalizer)
        local_out = segment_attention(q_part, k_part, v_part)
        mixed = head_rms(blend_weight * recalled + (1.0 - blend_weight) * local_out).astype(
            jnp.bfloat16
        )
        return (
            (
                seg_decay[:, None, None] * memory + update,
                seg_decay[:, None] * normalizer + key_total,
            ),
            mixed,
        )

    _, attended = lax.scan(
        one_segment,
        (prior_memory, prior_norm),
        (q_seg, k_seg, v_seg, local_decay, updates, key_sums),
    )
    attended = attended.reshape(seg_count * SEG, head_count * head_width)
    summary_state = summary
    row_count = summary.shape[0]
    for decode_step in range(STEPS):
        lifted = feature_map(
            jnp.dot(summary_state, wq_sum, preferred_element_type=jnp.float32).reshape(
                row_count, head_count, head_width
            )
        )
        recalled = head_rms(memory_read(lifted, final_memory, final_norm)).astype(jnp.bfloat16)
        partial_out = jnp.dot(
            recalled.reshape(row_count, head_count * head_width),
            wo_sum,
            preferred_element_type=jnp.float32,
        )
        summed = lax.psum(partial_out.astype(jnp.bfloat16), "sub").astype(jnp.float32)
        summary_state = (summary_state.astype(jnp.float32) + summed).astype(jnp.bfloat16)
    return (attended, summary_state)


def solution(mesh):
    placed = (
        P(("book", "seq"), "sub"),
        P(("book", "seq"), "sub"),
        P(("book", "seq"), "sub"),
        P("book", "sub"),
        P("sub"),
        P(("book", "seq"), None),
        P(None, "sub"),
        P("sub", None),
    )
    return jax.shard_map(
        on_device,
        mesh=mesh,
        in_specs=placed,
        out_specs=(P(("book", "seq"), "sub"), P(("book", "seq"), None)),
        check_vma=False,
    )
```

profile of v0, /device:TPU:0, one launch (start us, length us, event | category | flops | bytes accessed | tf_op | source)
XLA Modules:
  0.0 366.3 jit_solution(7190378475324766708)
XLA Ops:
  8.3 7.9 %fusion.73 = f32[2,256,256]{2,1,0:T(8,128)} fusion(bf16[256,2,8,256]{3,2,1,0:T(8,128)(2,1)} %bitcast.224, bf16[256,2,8,256]{3,2,1,0:T(8,128)(2,1)} %bitcast.186, f32[2]{0:T(128)S(1)} %broadcast_multiply_fusion), kind=kOutput, calls=%fused_computation.95 | convolution fusion | flops 3226599424 | bytes 4718600 | tf_op jit(solution)/shard_map/jqhd,jqhe->jhde/dot_general | solution.py:79
  17.9 2.7 fusion.170
  20.6 2.5 convert_element_type.126
  23.1 3.5 fusion.17
  29.3 6.4 %fusion.46 = f32[2,512,2048]{2,1,0:T(8,128)} fusion(bf16[512,2,256]{0,2,1:T(8,128)(2,1)} %bitcast.197, bf16[256,2,8,256]{3,2,1,0:T(8,128)(2,1)} %bitcast.187), kind=kOutput, calls=%fused_computation.76 | convolution fusion | flops 1073741824 | bytes 11010048 | tf_op jit(solution)/shard_map/while/body/eval_jaxpr/qhd,khd->hqk/dot_general | solution.py:52
  39.4 6.4 %fusion.48 = f32[2,512,2048]{2,1,0:T(8,128)} fusion(bf16[512,2,256]{0,2,1:T(8,128)(2,1)} %bitcast.198, bf16[256,2,8,256]{3,2,1,0:T(8,128)(2,1)} %bitcast.188), kind=kOutput, calls=%fused_computation.78 | convolution fusion | flops 1073741824 | bytes 11010048 | tf_op jit(solution)/shard_map/while/body/eval_jaxpr/qhd,khd->hqk/dot_general | solution.py:52
  49.4 6.4 %fusion.50 = f32[2,512,2048]{2,1,0:T(8,128)} fusion(bf16[512,2,256]{0,2,1:T(8,128)(2,1)} %bitcast.199, bf16[256,2,8,256]{3,2,1,0:T(8,128)(2,1)} %bitcast.189), kind=kOutput, calls=%fused_computation.80 | convolution fusion | flops 1073741824 | bytes 11010048 | tf_op jit(solution)/shard_map/while/body/eval_jaxpr/qhd,khd->hqk/dot_general | solution.py:52
  58.4 6.4 %fusion.52 = f32[2,512,2048]{2,1,0:T(8,128)} fusion(bf16[512,2,256]{0,2,1:T(8,128)(2,1)} %bitcast.200, bf16[256,2,8,256]{3,2,1,0:T(8,128)(2,1)} %bitcast.190), kind=kOutput, calls=%fused_computation.82 | convolution fusion | flops 1073741824 | bytes 11010048 | tf_op jit(solution)/shard_map/while/body/eval_jaxpr/qhd,khd->hqk/dot_general | solution.py:52
  65.4 6.1 %all-gather.1 = f32[4,1,2]{2,1,0:T(1,128)} all-gather(f32[1,1,2]{2,1,0:T(1,128)S(1)} %bitcast.214), channel_id=1, replica_groups=mesh['book'=2,'seq'=4,'sub'=4] {'seq'}, dimensions={0}, use_global_device_ids=true | all-gather | bytes 40 | tf_op jit(solution)/shard_map/all_gather | solution.py:13
  71.5 5.6 %all_gather.14 = f32[4,2,256]{2,1,0:T(2,128)S(1)} all-gather(f32[1,2,256]{2,1,0:T(2,128)S(1)} %broadcast_add_fusion), channel_id=1, replica_groups=mesh['book'=2,'seq'=4,'sub'=4] {'seq'}, dimensions={0}, use_global_device_ids=true | all-gather | bytes 10240 | tf_op jit(solution)/shard_map/all_gather | solution.py:13
  77.2 13.3 %fusion.171 = (f32[2,512]{1,0:T(2,128)S(1)}, f32[2,512,2048]{2,1,0:T(8,128)}) fusion(f32[2,512,2048]{2,1,0:T(8,128)} %fusion.46, pred[512,2048]{1,0:T(8,128)(4,1)} %iota_compare_fusion), kind=kOutput, calls=%fused_computation.225 | output fusion | flops 12584959 | bytes 17829888 | tf_op jit(solution)/shard_map/while/body/eval_jaxpr/sub | solution.py:62
  90.4 6.5 %fusion.61 = f32[512,2,256]{0,2,1:T(8,128)} fusion(f32[2,512,2048]{2,1,0:T(8,128)} %get-tuple-element.252, f32[2,512]{1,0:T(2,128)S(1)} %get-tuple-element.251, bf16[256,2,8,256]{3,2,1,0:T(8,128)(2,1)} %bitcast.225), kind=kOutput, calls=%fused_computation.91 | convolution fusion | flops 1077936128 | bytes 11538432 | tf_op jit(solution)/shard_map/while/body/eval_jaxpr/hqk,khd->qhd/dot_general | solution.py:64
  96.9 8.6 %fusion.172 = (f32[2,512]{1,0:T(2,128)S(1)}, f32[2,512,2048]{2,1,0:T(8,128)}) fusion(f32[2,512,2048]{2,1,0:T(8,128)S(1)} %bitcast.193, pred[512,2048]{1,0:T(8,128)(4,1)} %iota_compare_fusion.1), kind=kOutput, calls=%fused_computation.226 | output fusion | flops 12584959 | bytes 17829888 | tf_op jit(solution)/shard_map/while/body/eval_jaxpr/sub | solution.py:62
  105.5 6.5 %fusion.64 = f32[512,2,256]{0,2,1:T(8,128)} fusion(f32[2,512,2048]{2,1,0:T(8,128)} %get-tuple-element.254, f32[2,512]{1,0:T(2,128)S(1)} %get-tuple-element.253, bf16[256,2,8,256]{3,2,1,0:T(8,128)(2,1)} %bitcast.226), kind=kOutput, calls=%fused_computation.92 | convolution fusion | flops 1077936128 | bytes 11538432 | tf_op jit(solution)/shard_map/while/body/eval_jaxpr/hqk,khd->qhd/dot_general | solution.py:64
  112.0 13.2 %fusion.173 = (f32[2,512]{1,0:T(2,128)S(1)}, f32[2,512,2048]{2,1,0:T(8,128)}) fusion(f32[2,512,2048]{2,1,0:T(8,128)} %fusion.50, pred[512,2048]{1,0:T(8,128)(4,1)S(1)} %copy-done.6), kind=kOutput, calls=%fused_computation.227 | output fusion | flops 12584959 | bytes 17829888 | tf_op jit(solution)/shard_map/while/body/eval_jaxpr/sub | solution.py:62
  125.7 12.7 %fusion.174 = (f32[2,512]{1,0:T(2,128)S(1)}, f32[2,512,2048]{2,1,0:T(8,128)}) fusion(f32[2,512,2048]{2,1,0:T(8,128)} %fusion.52, pred[512,2048]{1,0:T(8,128)(4,1)S(1)} %copy-done.5), kind=kOutput, calls=%fused_computation.228 | output fusion | flops 12584959 | bytes 17829888 | tf_op jit(solution)/shard_map/while/body/eval_jaxpr/sub | solution.py:62
  138.4 6.0 %fusion.67 = f32[512,2,256]{0,2,1:T(8,128)} fusion(f32[2,512,2048]{2,1,0:T(8,128)} %get-tuple-element.256, f32[2,512]{1,0:T(2,128)S(1)} %get-tuple-element.255, bf16[256,2,8,256]{3,2,1,0:T(8,128)(2,1)S(1)} %bitcast.227), kind=kOutput, calls=%fused_computation.93 | convolution fusion | flops 1077936128 | bytes 11538432 | tf_op jit(solution)/shard_map/while/body/eval_jaxpr/hqk,khd->qhd/dot_general | solution.py:64
  144.5 2.5 fusion.70
  147.0 5.9 %while.10 = (s32[]{:T(128)}, f32[2,256,256]{2,1,0:T(8,128)S(1)}, f32[2,256]{1,0:T(2,128)S(1)}, s32[]{:T(128)}, f32[4,2]{1,0:T(4,128)}, /*index=5*/f32[4,2,256,25...) while((s32[]{:T(128)}, f32[2,256,256]{2,1,0:T(8,128)S(1)}, f32[2,256]{1,0:T(2,128)S(1)}, ...), condition=%wide.region_2.3_spmd.clone, body=%wide.region_1.2_spmd.clone.sunk | while | flops 526340 | bytes 1579175 | solution.py:22
  153.7 7.3 %psum.43 = f32[2,256]{1,0:T(2,128)S(1)} all-reduce(f32[2,256]{1,0:T(2,128)S(1)} %add_select_fusion.1), channel_id=1, replica_groups=mesh['book'=2,'seq'=4,'sub'=4] {'seq'}, use_global_device_ids=true, to_apply=%region_13.14 | all-reduce | flops 512 | bytes 4096 | tf_op jit(solution)/shard_map/psum | solution.py:27
  162.8 7.0 %fusion.38 = f32[2,1,2048]{2,1,0:T(1,128)S(1)} fusion(f32[256,2,8,256]{3,2,1,0:T(8,128)} %bitcast.194, f32[2,256,1]{1,0,2:T(2,128)S(1)} %bitcast.213), kind=kOutput, calls=%fused_computation.66 | convolution fusion | flops 16777216 | bytes 4212736 | tf_op jit(solution)/shard_map/while/body/eval_jaxpr/qhd,hd->qh/dot_general | solution.py:40
  170.1 26.2 %all-reduce.6.cloned.1.call-done = f32[2,256,256]{2,1,0:T(8,128)} async-done(((f32[2,256,256]{2,1,0:T(8,128)}), f32[2,256,256]{2,1,0:T(8,128)}) %all-reduce.6.cloned.1.call-update) | async-done | bytes 524304 | tf_op jit(solution)/shard_map/psum | solution.py:27
  199.3 35.4 %all-reduce.8.cloned.1.call-done = bf16[64,2048]{1,0:T(8,128)(2,1)} async-done(((bf16[64,2048]{1,0:T(8,128)(2,1)}), bf16[64,2048]{1,0:T(8,128)(2,1)}) %all-reduce.8.cloned.1.call-update) | async-done | bytes 262160 | tf_op jit(solution)/shard_map/psum | solution.py:157
  234.7 2.1 fusion.100
  240.4 17.1 %multiply_reduce_fusion = (f32[2048,2]{0,1:T(2,128)S(1)}, f32[2048,2,256]{0,2,1:T(8,128)}) fusion(f32[512,2,256]{0,2,1:T(8,128)} %fusion.61, f32[512,2,256]{0,2,1:T(8,128)} %fusion.64, f32[512,2,256]{0,2,1:T(8,128)} %fusion.67, f32[512,2,256]{0,2,1:T(8,128)} %fusion.70, f32[2]{0:T(128)S(1)} %copy-done.13, f32[2048,2]{0,1:T(2,128)S(1)} %fusion.134, ...), kind=kOutput, calls=%fused_computation.45 | convolution fusion | flops 3234852864 | bytes 13139984 | tf_op jit(solution)/shard_map/while/body/eval_jaxpr/qhd,hde->qhe/dot_general | solution.py:39
  257.5 17.8 %all-reduce.10.cloned.1.call-done = bf16[64,2048]{1,0:T(8,128)(2,1)} async-done(((bf16[64,2048]{1,0:T(8,128)(2,1)}), bf16[64,2048]{1,0:T(8,128)(2,1)}) %all-reduce.10.cloned.1.call-update) | async-done | bytes 262160 | tf_op jit(solution)/shard_map/psum | solution.py:157
  276.4 2.1 fusion.176
  281.7 35.2 %all-reduce.12.cloned.1.call-done = bf16[64,2048]{1,0:T(8,128)(2,1)} async-done(((bf16[64,2048]{1,0:T(8,128)(2,1)}), bf16[64,2048]{1,0:T(8,128)(2,1)}) %all-reduce.12.cloned.1.call-update) | async-done | bytes 262160 | tf_op jit(solution)/shard_map/psum | solution.py:157
  316.9 2.1 fusion.101
  322.3 4.1 %multiply_convert_fusion = bf16[2048,2,256]{0,2,1:T(8,128)(2,1)} fusion(f32[2048,2,256]{0,2,1:T(8,128)} %get-tuple-element.260, f32[2048,2]{0,1:T(2,128)S(1)} %add_rsqrt_fusion), kind=kLoop, calls=%fused_computation.44 | loop fusion | flops 2097152 | bytes 6307840 | tf_op jit(solution)/shard_map/while/body/eval_jaxpr/convert_element_type | solution.py:126
  326.3 3.9 %copy.135 = bf16[2048,512]{1,0:T(8,128)(2,1)} copy(bf16[2048,512]{0,1:T(8,128)(2,1)} %bitcast.191) | data formatting | bytes 4194304
  330.3 27.2 %all-reduce.14.cloned.1.call-done = bf16[64,2048]{1,0:T(8,128)(2,1)} async-done(((bf16[64,2048]{1,0:T(8,128)(2,1)}), bf16[64,2048]{1,0:T(8,128)(2,1)}) %all-reduce.14.cloned.1.call-update) | async-done | bytes 262160 | tf_op jit(solution)/shard_map/psum | solution.py:157
  (113 shorter events, 41.1 us)
Async XLA Ops:
  7.2 190.9 %copy-start = (bf16[512,2048]{1,0:T(8,128)(2,1)S(1)}, bf16[512,2048]{1,0:T(8,128)(2,1)}, u32[]{:S(2)}) copy-start(bf16[512,2048]{1,0:T(8,128)(2,1)} %param.17) | copy-start | bytes 6291460
  7.2 139.8 %all-gather.4.cloned.1.call-start = ((), (), s32[]{:S(2)}) async-start(), calls=%async_computation.5 | async-start | bytes 2621440 | tf_op jit(solution)/shard_map/all_gather | solution.py:13
  8.2 57.1 %copy-start.9 = (f32[2]{0:T(128)}, f32[2]{0:T(128)S(1)}, u32[]{:S(2)}) copy-start(f32[2]{0:T(128)S(1)} %dynamic-slice_reduce_fusion) | copy-start | bytes 28
  8.2 63.2 %copy-start.10 = (f32[2]{0:T(128)}, f32[2]{0:T(128)S(1)}, u32[]{:S(2)}) copy-start(f32[2]{0:T(128)S(1)} %broadcast_multiply_fusion) | copy-start | bytes 28
  16.2 180.1 %all-reduce.6.cloned.1.call-start = ((), (), s32[]{:S(2)}) async-start(), calls=%async_computation | async-start | bytes 1048576 | tf_op jit(solution)/shard_map/psum | solution.py:27
  16.4 4.2 %copy-start.2 = (bf16[2048,512]{1,0:T(8,128)(2,1)S(1)}, bf16[2048,512]{1,0:T(8,128)(2,1)}, u32[]{:S(2)}) copy-start(bf16[2048,512]{1,0:T(8,128)(2,1)} %param.10) | copy-start | bytes 6291460
  58.4 6.4 %copy-start.12 = (f32[2]{0:T(128)S(1)}, f32[2]{0:T(128)}, u32[]{:S(2)}) copy-start(f32[2]{0:T(128)} %param.14) | copy-start | bytes 28
  77.1 19.8 %slice-start = ((s8[8388608]{0:T(1024)(128)(4,1)}), s8[4194304]{0:T(1024)(128)(4,1)S(1)}, s32[]{:S(2)}) async-start(s8[8388608]{0:T(1024)(128)(4,1)} %bitcast.192), calls=%async_computation.6 | async-start | bytes 8388608
  90.4 6.5 %slice-start.1 = ((s8[8388608]{0:T(1024)(128)(4,1)}), s8[4194304]{0:T(1024)(128)(4,1)S(1)}, s32[]{:S(2)}) async-start(s8[8388608]{0:T(1024)(128)(4,1)} %bitcast.192), calls=%async_computation.7 | async-start | bytes 8388608
  105.5 6.5 %copy-start.6 = (pred[512,2048]{1,0:T(8,128)(4,1)S(1)}, pred[512,2048]{1,0:T(8,128)(4,1)}, u32[]{:S(2)}) copy-start(pred[512,2048]{1,0:T(8,128)(4,1)} %iota_compare_fusion.2) | copy-start | bytes 3145732
  112.0 13.2 %copy-start.1 = (bf16[2048,512]{1,0:T(8,128)(2,1)S(1)}, bf16[2048,512]{1,0:T(8,128)(2,1)}, u32[]{:S(2)}) copy-start(bf16[2048,512]{1,0:T(8,128)(2,1)} %param.16) | copy-start | bytes 6291460
  112.0 13.2 %copy-start.3 = (bf16[64,2048]{1,0:T(8,128)(2,1)S(1)}, bf16[64,2048]{1,0:T(8,128)(2,1)}, u32[]{:S(2)}) copy-start(bf16[64,2048]{1,0:T(8,128)(2,1)} %param.15) | copy-start | bytes 786436
  112.0 13.7 %copy-start.5 = (pred[512,2048]{1,0:T(8,128)(4,1)S(1)}, pred[512,2048]{1,0:T(8,128)(4,1)}, u32[]{:S(2)}) copy-start(pred[512,2048]{1,0:T(8,128)(4,1)} %iota_compare_fusion.3) | copy-start | bytes 3145732
  125.7 12.8 %copy-start.11 = (bf16[2048,512]{1,0:T(8,128)(2,1)S(1)}, bf16[2048,512]{1,0:T(8,128)(2,1)}, u32[]{:S(2)}) copy-start(bf16[2048,512]{1,0:T(8,128)(2,1)} %param.12) | copy-start | bytes 6291460
  138.4 6.0 %copy-start.15 = (f32[2,512,2048]{2,1,0:T(8,128)S(1)}, f32[2,512,2048]{2,1,0:T(8,128)}, u32[]{:S(2)}) copy-start(f32[2,512,2048]{2,1,0:T(8,128)} %get-tuple-element.258) | copy-start | bytes 25165828
  147.0 14.0 %copy-start.4 = (f32[2,256,256]{2,1,0:T(8,128)S(1)}, f32[2,256,256]{2,1,0:T(8,128)}, u32[]{:S(2)}) copy-start(f32[2,256,256]{2,1,0:T(8,128)} %fusion.73) | copy-start | bytes 1572868
  162.6 72.1 %all-reduce.8.cloned.1.call-start = ((), (), s32[]{:S(2)}) async-start(), calls=%async_computation.1 | async-start | bytes 524288 | tf_op jit(solution)/shard_map/psum | solution.py:157
  199.2 41.1 %copy-start.13 = (f32[2]{0:T(128)S(1)}, f32[2]{0:T(128)}, u32[]{:S(2)}) copy-start(f32[2]{0:T(128)} %get-tuple-element.245) | copy-start | bytes 28
  199.2 41.1 %copy-start.14 = (f32[2]{0:T(128)S(1)}, f32[2]{0:T(128)}, u32[]{:S(2)}) copy-start(f32[2]{0:T(128)} %get-tuple-element.246) | copy-start | bytes 28
  199.3 76.0 %all-reduce.10.cloned.1.call-start = ((), (), s32[]{:S(2)}) async-start(), calls=%async_computation.2 | async-start | bytes 524288 | tf_op jit(solution)/shard_map/psum | solution.py:157
  240.1 76.8 %all-reduce.12.cloned.1.call-start = ((), (), s32[]{:S(2)}) async-start(), calls=%async_computation.3 | async-start | bytes 524288 | tf_op jit(solution)/shard_map/psum | solution.py:157
  240.4 34.9 %copy-start.7 = (bf16[64,2048]{1,0:T(8,128)(2,1)S(1)}, bf16[64,2048]{1,0:T(8,128)(2,1)}, u32[]{:S(2)}) copy-start(bf16[64,2048]{1,0:T(8,128)(2,1)} %all-reduce.8.cloned.1.call-done) | copy-start | bytes 786436
  281.7 75.8 %all-reduce.14.cloned.1.call-start = ((), (), s32[]{:S(2)}) async-start(), calls=%async_computation.4 | async-start | bytes 524288 | tf_op jit(solution)/shard_map/psum | solution.py:157
  322.3 35.2 %copy-start.8 = (bf16[64,2048]{1,0:T(8,128)(2,1)S(1)}, bf16[64,2048]{1,0:T(8,128)(2,1)}, u32[]{:S(2)}) copy-start(bf16[64,2048]{1,0:T(8,128)(2,1)} %all-reduce.12.cloned.1.call-done) | copy-start | bytes 786436
Sparse Core Ops, SparseCore 0:
  16.3 25.2 all-gather.3
  162.7 33.5 all-reduce.5
  199.4 35.3 all-reduce.7
  240.2 35.0 all-reduce.9
  281.8 35.0 all-reduce.11
  322.4 35.0 all-reduce.13
where the time goes:
time: 372 us; the launch traced here: 366 us
  waiting for transfers between devices  142 us (38%)
  matrix products  98.1 us (26%)
  other arithmetic  74.2 us (20%)
  blocking collectives  19 us (5%)
  local copies, waits for them, and re-layouts  17.6 us (5%)
  between operations  14.6 us (4%)
    psum x4, waiting for transfers between devices, on_device(): lax.psum(partial_out.astype(jnp.bfloat16), 'sub').astype(jnp.float32)  116 us
    sub x4, other arithmetic, segment_attention(): weights = jax.nn.softmax(scores, axis=-1).astype(jnp.bfloat16)  47.7 us
    psum x1, waiting for transfers between devices, broadcast(): return lax.psum(jnp.where(mine, x, jnp.zeros_like(x)), axis)  26.2 us
    dot_general x4, matrix products, segment_attention(): jnp.einsum('qhd,khd->hqk', q_part[first_row:first_row + block_rows], k_pa...  25.5 us
    dot_general x5, matrix products, memory_read(): jnp.einsum('qhd,hde->qhe', lifted, memory, precision=top_precision)  23.6 us
    dot_general x4, matrix products, segment_attention(): jnp.einsum('hqk,khd->qhd', weights, v_part, preferred_element_type=jnp.fl...  21.6 us
    all_gather x2, blocking collectives, carried_in(): pieces = jax.tree.map(lambda part: lax.all_gather(part, axis), value)  11.7 us
    unnamed x41, local copies, waits for them, and re-layouts  11.2 us
  transfers between devices with their start and end apart: 6, of which 5 were waited for; matrix products, arithmetic and copies ran while one was open for 41% of the time, Pallas kernels for 0%

commit v1 on v0

--- a/solution.py
+++ b/solution.py
@@ -2,10 +2,15 @@
 import jax.numpy as jnp
 from jax import lax
 from jax.sharding import PartitionSpec as P
+from jax.lax import all_gather
 
 SEG = 2048
 STEPS = 4
 top_precision = lax.Precision.HIGHEST
+
+
+def _replace_results(block_here):
+    return jnp.sum(all_gather(block_here, axis_name="sub"), 0)
 
 
 def carried_in(value, axis, join, neutral):
@@ -154,7 +159,7 @@
             wo_sum,
             preferred_element_type=jnp.float32,
         )
-        summed = lax.psum(partial_out.astype(jnp.bfloat16), "sub").astype(jnp.float32)
+        summed = _replace_results(partial_out.astype(jnp.bfloat16)).astype(jnp.float32)
         summary_state = (summary_state.astype(jnp.float32) + summed).astype(jnp.bfloat16)
     return (attended, summary_state)
 

time: 372 us -> 305 us (0.82)
  waiting for transfers between devices: 142 us -> 74.4 us
    psum x4 -> x0, waiting for transfers between devices: 116 us -> none  [on_device(): lax.psum(partial_out.astype(jnp.bfloat16), 'sub').astype(jnp.float32)]
    all_gather x0 -> x4, waiting for transfers between devices: none -> 41 us  [_replace_results(): return jnp.sum(all_gather(block_here, axis_name='sub'), 0)]
    psum x1, waiting for transfers between devices: 26.2 us -> 33.3 us  [broadcast(): return lax.psum(jnp.where(mine, x, jnp.zeros_like(x)), axis)]
    reduce_sum x0 -> x4, other arithmetic: none -> 6.37 us  [_replace_results(): return jnp.sum(all_gather(block_here, axis_name='sub'), 0)]
    unnamed x41 -> x27, local copies, waits for them, and re-layouts: 11.2 us -> 13.1 us
  transfers between devices with their start and end apart: 6 -> 6, of which waited for: 5 -> 5; matrix products, arithmetic and copies ran while one was open for 41% -> 49% of each run, Pallas kernels for 0% -> 0%
where the time goes in v1:
time: 305 us; the launch traced here: 300 us
  matrix products  98.4 us (32%)
  other arithmetic  75.5 us (25%)
  waiting for transfers between devices  74.4 us (24%)
  blocking collectives  19 us (6%)
  local copies, waits for them, and re-layouts  16.9 us (6%)
  between operations  14.7 us (5%)
    sub x4, other arithmetic, segment_attention(): weights = jax.nn.softmax(scores, axis=-1).astype(jnp.bfloat16)  48.6 us
    all_gather x4, waiting for transfers between devices, _replace_results(): return jnp.sum(all_gather(block_here, axis_name='sub'), 0)  41 us
    psum x1, waiting for transfers between devices, broadcast(): return lax.psum(jnp.where(mine, x, jnp.zeros_like(x)), axis)  33.3 us
    dot_general x4, matrix products, segment_attention(): jnp.einsum('qhd,khd->hqk', q_part[first_row:first_row + block_rows], k_pa...  25.8 us
    dot_general x4, matrix products, segment_attention(): jnp.einsum('hqk,khd->qhd', weights, v_part, preferred_element_type=jnp.fl...  25 us
    dot_general x5, matrix products, memory_read(): jnp.einsum('qhd,hde->qhe', lifted, memory, precision=top_precision)  22.6 us
    unnamed x27, local copies, waits for them, and re-layouts  13.1 us
    all_gather x2, blocking collectives, carried_in(): pieces = jax.tree.map(lambda part: lax.all_gather(part, axis), value)  11.8 us
  transfers between devices with their start and end apart: 6, of which 5 were waited for; matrix products, arithmetic and copies ran while one was open for 49% of the time, Pallas kernels for 0%

profile of v1, /device:TPU:0, one launch (start us, length us, event | category | flops | bytes accessed | tf_op | source)
XLA Modules:
  0.0 300.0 jit_solution(10122963186352952920)
XLA Ops:
  8.2 7.9 %fusion.73 = f32[2,256,256]{2,1,0:T(8,128)} fusion(bf16[256,2,8,256]{3,2,1,0:T(8,128)(2,1)} %bitcast.232, bf16[256,2,8,256]{3,2,1,0:T(8,128)(2,1)} %bitcast.190, f32[2]{0:T(128)S(1)} %broadcast_multiply_fusion), kind=kOutput, calls=%fused_computation.95 | convolution fusion | flops 3226599424 | bytes 4718600 | tf_op jit(solution)/shard_map/jqhd,jqhe->jhde/dot_general | solution.py:84
  16.4 3.5 %fusion.17 = f32[512]{0:T(512)S(1)} fusion(bf16[2048,512]{1,0:T(8,128)(2,1)} %param.11), kind=kLoop, calls=%fused_computation.37 | loop fusion | flops 6290944 | bytes 2099200 | tf_op jit(solution)/shard_map/reduce_sum | solution.py:87
  19.9 2.7 fusion.170
  22.6 2.1 copy.157
  24.7 6.6 %fusion.46 = f32[2,512,2048]{2,1,0:T(8,128)} fusion(bf16[512,2,256]{0,2,1:T(8,128)(2,1)} %bitcast.202, bf16[256,2,8,256]{3,2,1,0:T(8,128)(2,1)} %bitcast.191), kind=kOutput, calls=%fused_computation.76 | convolution fusion | flops 1073741824 | bytes 11010048 | tf_op jit(solution)/shard_map/while/body/eval_jaxpr/qhd,khd->hqk/dot_general | solution.py:57
  32.9 2.1 copy.156
  34.9 6.4 %fusion.48 = f32[2,512,2048]{2,1,0:T(8,128)} fusion(bf16[512,2,256]{0,2,1:T(8,128)(2,1)} %bitcast.203, bf16[256,2,8,256]{3,2,1,0:T(8,128)(2,1)} %bitcast.192), kind=kOutput, calls=%fused_computation.78 | convolution fusion | flops 1073741824 | bytes 11010048 | tf_op jit(solution)/shard_map/while/body/eval_jaxpr/qhd,khd->hqk/dot_general | solution.py:57
  45.0 6.4 %fusion.50 = f32[2,512,2048]{2,1,0:T(8,128)} fusion(bf16[512,2,256]{0,2,1:T(8,128)(2,1)} %bitcast.204, bf16[256,2,8,256]{3,2,1,0:T(8,128)(2,1)} %bitcast.193), kind=kOutput, calls=%fused_computation.80 | convolution fusion | flops 1073741824 | bytes 11010048 | tf_op jit(solution)/shard_map/while/body/eval_jaxpr/qhd,khd->hqk/dot_general | solution.py:57
  54.0 6.1 %all-gather.5 = f32[4,1,2]{2,1,0:T(1,128)S(1)} all-gather(f32[1,1,2]{2,1,0:T(1,128)S(1)} %bitcast.222), channel_id=1, replica_groups=mesh['book'=2,'seq'=4,'sub'=4] {'seq'}, dimensions={0}, use_global_device_ids=true | all-gather | bytes 40 | tf_op jit(solution)/shard_map/all_gather | solution.py:18
  60.2 5.6 %all_gather.38 = f32[4,2,256]{2,1,0:T(2,128)S(1)} all-gather(f32[1,2,256]{2,1,0:T(2,128)S(1)} %broadcast_add_fusion), channel_id=1, replica_groups=mesh['book'=2,'seq'=4,'sub'=4] {'seq'}, dimensions={0}, use_global_device_ids=true | all-gather | bytes 10240 | tf_op jit(solution)/shard_map/all_gather | solution.py:18
  65.8 13.3 %fusion.171 = (f32[2,512]{1,0:T(2,128)S(1)}, f32[2,512,2048]{2,1,0:T(8,128)}) fusion(f32[2,512,2048]{2,1,0:T(8,128)} %fusion.46, pred[512,2048]{1,0:T(8,128)(4,1)} %iota_compare_fusion), kind=kOutput, calls=%fused_computation.225 | output fusion | flops 12584959 | bytes 17829888 | tf_op jit(solution)/shard_map/while/body/eval_jaxpr/sub | solution.py:67
  79.6 13.4 %fusion.172 = (f32[2,512]{1,0:T(2,128)S(1)}, f32[2,512,2048]{2,1,0:T(8,128)}) fusion(f32[2,512,2048]{2,1,0:T(8,128)} %fusion.48, pred[512,2048]{1,0:T(8,128)(4,1)} %iota_compare_fusion.1), kind=kOutput, calls=%fused_computation.226 | output fusion | flops 12584959 | bytes 17829888 | tf_op jit(solution)/shard_map/while/body/eval_jaxpr/sub | solution.py:67
  93.0 8.5 %fusion.173 = (f32[2,512]{1,0:T(2,128)S(1)}, f32[2,512,2048]{2,1,0:T(8,128)}) fusion(f32[2,512,2048]{2,1,0:T(8,128)S(1)} %bitcast.197, pred[512,2048]{1,0:T(8,128)(4,1)} %iota_compare_fusion.2), kind=kOutput, calls=%fused_computation.227 | output fusion | flops 12584959 | bytes 17829888 | tf_op jit(solution)/shard_map/while/body/eval_jaxpr/sub | solution.py:67
  101.5 6.6 %fusion.61 = f32[512,2,256]{0,2,1:T(8,128)} fusion(f32[2,512,2048]{2,1,0:T(8,128)} %get-tuple-element.252, f32[2,512]{1,0:T(2,128)S(1)} %get-tuple-element.251, bf16[256,2,8,256]{3,2,1,0:T(8,128)(2,1)} %bitcast.233), kind=kOutput, calls=%fused_computation.91 | convolution fusion | flops 1077936128 | bytes 11538432 | tf_op jit(solution)/shard_map/while/body/eval_jaxpr/hqk,khd->qhd/dot_general | solution.py:69
  108.1 3.8 %while.10 = (s32[]{:T(128)}, f32[2,256,256]{2,1,0:T(8,128)S(1)}, f32[2,256]{1,0:T(2,128)S(1)}, s32[]{:T(128)}, f32[4,2]{1,0:T(4,128)S(1)}, /*index=5*/f32[4,2,25...) while((s32[]{:T(128)}, f32[2,256,256]{2,1,0:T(8,128)S(1)}, ...), condition=%wide.region_2.3_spmd.clone, body=%wide.region_1.2_spmd.clone.sunk | while | flops 526340 | bytes 1579175 | solution.py:27
  112.0 7.3 %psum.15 = f32[2,256]{1,0:T(2,128)S(1)} all-reduce(f32[2,256]{1,0:T(2,128)S(1)} %add_select_fusion.1), channel_id=1, replica_groups=mesh['book'=2,'seq'=4,'sub'=4] {'seq'}, use_global_device_ids=true, to_apply=%region_13.14 | all-reduce | flops 512 | bytes 4096 | tf_op jit(solution)/shard_map/psum | solution.py:32
  121.5 33.3 %all-reduce.2.cloned.1.call-done = f32[2,256,256]{2,1,0:T(8,128)} async-done(((f32[2,256,256]{2,1,0:T(8,128)}), f32[2,256,256]{2,1,0:T(8,128)}) %all-reduce.2.cloned.1.call-update) | async-done | bytes 524304 | tf_op jit(solution)/shard_map/psum | solution.py:32
  157.9 6.5 %fusion.52 = f32[2,512,2048]{2,1,0:T(8,128)} fusion(bf16[512,2,256]{0,2,1:T(8,128)(2,1)} %bitcast.201, bf16[256,2,8,256]{3,2,1,0:T(8,128)(2,1)} %bitcast.194), kind=kOutput, calls=%fused_computation.82 | convolution fusion | flops 1073741824 | bytes 11010048 | tf_op jit(solution)/shard_map/while/body/eval_jaxpr/qhd,khd->hqk/dot_general | solution.py:57
  165.9 6.0 %fusion.64 = f32[512,2,256]{0,2,1:T(8,128)} fusion(f32[2,512,2048]{2,1,0:T(8,128)} %get-tuple-element.254, f32[2,512]{1,0:T(2,128)S(1)} %get-tuple-element.253, bf16[256,2,8,256]{3,2,1,0:T(8,128)(2,1)S(1)} %bitcast.235), kind=kOutput, calls=%fused_computation.92 | convolution fusion | flops 1077936128 | bytes 11538432 | tf_op jit(solution)/shard_map/while/body/eval_jaxpr/hqk,khd->qhd/dot_general | solution.py:69
  171.8 14.1 %all-gather.14.cloned.1.call-done = bf16[256,2048]{1,0:T(8,128)(2,1)} async-done(((bf16[64,2048]{1,0:T(8,128)(2,1)}), bf16[256,2048]{1,0:T(8,128)(2,1)}) %all-gather.14.cloned.1.call-update) | async-done | bytes 1048592 | tf_op jit(solution)/shard_map/all_gather | solution.py:13
  187.3 2.1 fusion.100
  193.2 13.4 %fusion.174 = (f32[2,512]{1,0:T(2,128)S(1)}, f32[2,512,2048]{2,1,0:T(8,128)}) fusion(f32[2,512,2048]{2,1,0:T(8,128)} %fusion.52, pred[512,2048]{1,0:T(8,128)(4,1)} %iota_compare_fusion.3), kind=kOutput, calls=%fused_computation.228 | output fusion | flops 12584959 | bytes 17829888 | tf_op jit(solution)/shard_map/while/body/eval_jaxpr/sub | solution.py:67
  206.6 5.9 %fusion.67 = f32[512,2,256]{0,2,1:T(8,128)} fusion(f32[2,512,2048]{2,1,0:T(8,128)} %get-tuple-element.256, f32[2,512]{1,0:T(2,128)S(1)} %get-tuple-element.255, bf16[256,2,8,256]{3,2,1,0:T(8,128)(2,1)S(1)} %bitcast.236), kind=kOutput, calls=%fused_computation.93 | convolution fusion | flops 1077936128 | bytes 11538432 | tf_op jit(solution)/shard_map/while/body/eval_jaxpr/hqk,khd->qhd/dot_general | solution.py:69
  212.6 7.7 %all-gather.16.cloned.1.call-done = bf16[256,2048]{1,0:T(8,128)(2,1)} async-done(((bf16[64,2048]{1,0:T(8,128)(2,1)}), bf16[256,2048]{1,0:T(8,128)(2,1)}) %all-gather.16.cloned.1.call-update) | async-done | bytes 1048592 | tf_op jit(solution)/shard_map/all_gather | solution.py:13
  220.3 2.2 reduce_sum.155
  223.6 2.1 fusion.176
  229.1 6.5 %fusion.70 = f32[512,2,256]{0,2,1:T(8,128)} fusion(f32[2,512,2048]{2,1,0:T(8,128)} %get-tuple-element.258, f32[2,512]{1,0:T(2,128)S(1)} %get-tuple-element.257, bf16[256,2,8,256]{3,2,1,0:T(8,128)(2,1)} %bitcast.234), kind=kOutput, calls=%fused_computation.94 | convolution fusion | flops 1077936128 | bytes 11538432 | tf_op jit(solution)/shard_map/while/body/eval_jaxpr/hqk,khd->qhd/dot_general | solution.py:69
  238.2 4.8 %fusion.38 = f32[2,1,2048]{2,1,0:T(1,128)S(1)} fusion(f32[256,2,8,256]{3,2,1,0:T(8,128)S(1)} %bitcast.198, f32[2,256,1]{1,0,2:T(2,128)S(1)} %bitcast.221), kind=kOutput, calls=%fused_computation.66 | convolution fusion | flops 16777216 | bytes 4212736 | tf_op jit(solution)/shard_map/while/body/eval_jaxpr/qhd,hd->qh/dot_general | solution.py:45
  243.0 13.5 %all-gather.18.cloned.1.call-done = bf16[256,2048]{1,0:T(8,128)(2,1)} async-done(((bf16[64,2048]{1,0:T(8,128)(2,1)}), bf16[256,2048]{1,0:T(8,128)(2,1)}) %all-gather.18.cloned.1.call-update) | async-done | bytes 1048592 | tf_op jit(solution)/shard_map/all_gather | solution.py:13
  263.1 16.1 %multiply_reduce_fusion = (f32[2048,2]{0,1:T(2,128)S(1)}, f32[2048,2,256]{0,2,1:T(8,128)S(1)}) fusion(f32[512,2,256]{0,2,1:T(8,128)} %fusion.61, f32[512,2,256]{0,2,1:T(8,128)} %fusion.64, f32[512,2,256]{0,2,1:T(8,128)} %fusion.67, f32[512,2,256]{0,2,1:T(8,128)} %fusion.70, f32[2]{0:T(128)S(1)} %get-tuple-element.245, f32[2048,2]{0,1:T(2,128)S(1)} %fusion.134, ...), kind=kOutput, calls=%fused_computation.45 | convolution fusion | flops 3234852864 | bytes 13139984 | tf_op jit(solution)/shard_map/while/body/eval_jaxpr/qhd,hde->qhe/dot_general | solution.py:44
  281.1 3.9 %copy.135 = bf16[2048,512]{1,0:T(8,128)(2,1)} copy(bf16[2048,512]{0,1:T(8,128)(2,1)} %bitcast.195) | data formatting | bytes 4194304
  285.0 5.7 %all-gather.20.cloned.1.call-done = bf16[256,2048]{1,0:T(8,128)(2,1)} async-done(((bf16[64,2048]{1,0:T(8,128)(2,1)}), bf16[256,2048]{1,0:T(8,128)(2,1)}) %all-gather.20.cloned.1.call-update) | async-done | bytes 1048592 | tf_op jit(solution)/shard_map/all_gather | solution.py:13
  (103 shorter events, 43.4 us)
Async XLA Ops:
  7.2 149.4 %copy-start = (bf16[512,2048]{1,0:T(8,128)(2,1)S(1)}, bf16[512,2048]{1,0:T(8,128)(2,1)}, u32[]{:S(2)}) copy-start(bf16[512,2048]{1,0:T(8,128)(2,1)} %param.17) | copy-start | bytes 6291460
  7.2 100.9 %all-gather.12.cloned.1.call-start = ((), (), s32[]{:S(2)}) async-start(), calls=%async_computation.1 | async-start | bytes 2621440 | tf_op jit(solution)/shard_map/all_gather | solution.py:18
  16.1 138.7 %all-reduce.2.cloned.1.call-start = ((), (), s32[]{:S(2)}) async-start(), calls=%async_computation | async-start | bytes 1048576 | tf_op jit(solution)/shard_map/psum | solution.py:32
  65.8 13.3 %copy-start.1 = (bf16[2048,512]{1,0:T(8,128)(2,1)S(1)}, bf16[2048,512]{1,0:T(8,128)(2,1)}, u32[]{:S(2)}) copy-start(bf16[2048,512]{1,0:T(8,128)(2,1)} %param.16) | copy-start | bytes 6291460
  65.8 13.3 %copy-start.4 = (bf16[64,2048]{1,0:T(8,128)(2,1)S(1)}, bf16[64,2048]{1,0:T(8,128)(2,1)}, u32[]{:S(2)}) copy-start(bf16[64,2048]{1,0:T(8,128)(2,1)} %param.15) | copy-start | bytes 786436
  79.1 13.9 %slice-start = ((s8[8388608]{0:T(1024)(128)(4,1)}), s8[4194304]{0:T(1024)(128)(4,1)S(1)}, s32[]{:S(2)}) async-start(s8[8388608]{0:T(1024)(128)(4,1)} %bitcast.196), calls=%async_computation.6 | async-start | bytes 8388608
  79.6 13.4 %slice-start.1 = ((s8[8388608]{0:T(1024)(128)(4,1)}), s8[4194304]{0:T(1024)(128)(4,1)S(1)}, s32[]{:S(2)}) async-start(s8[8388608]{0:T(1024)(128)(4,1)} %bitcast.196), calls=%async_computation.7 | async-start | bytes 8388608
  121.2 64.7 %all-gather.14.cloned.1.call-start = ((), (), s32[]{:S(2)}) async-start(), calls=%async_computation.2 | async-start | bytes 1310720 | tf_op jit(solution)/shard_map/all_gather | solution.py:13
  157.8 62.5 %all-gather.16.cloned.1.call-start = ((), (), s32[]{:S(2)}) async-start(), calls=%async_computation.3 | async-start | bytes 1310720 | tf_op jit(solution)/shard_map/all_gather | solution.py:13
  157.9 8.0 %copy-start.6 = (bf16[2048,512]{1,0:T(8,128)(2,1)S(1)}, bf16[2048,512]{1,0:T(8,128)(2,1)}, u32[]{:S(2)}) copy-start(bf16[2048,512]{1,0:T(8,128)(2,1)} %param.12) | copy-start | bytes 6291460
  187.3 19.3 %copy-start.5 = (bf16[64,2048]{1,0:T(8,128)(2,1)}, bf16[64,2048]{1,0:T(8,128)(2,1)S(1)}, u32[]{:S(2)}) copy-start(bf16[64,2048]{1,0:T(8,128)(2,1)S(1)} %reduce_sum.153) | copy-start | bytes 786436
  192.7 63.8 %all-gather.18.cloned.1.call-start = ((), (), s32[]{:S(2)}) async-start(), calls=%async_computation.4 | async-start | bytes 1310720 | tf_op jit(solution)/shard_map/all_gather | solution.py:13
  193.2 13.4 %copy-start.7 = (bf16[2048,512]{1,0:T(8,128)(2,1)S(1)}, bf16[2048,512]{1,0:T(8,128)(2,1)}, u32[]{:S(2)}) copy-start(bf16[2048,512]{1,0:T(8,128)(2,1)} %param.12) | copy-start | bytes 6291460
  228.9 61.8 %all-gather.20.cloned.1.call-start = ((), (), s32[]{:S(2)}) async-start(), calls=%async_computation.5 | async-start | bytes 1310720 | tf_op jit(solution)/shard_map/all_gather | solution.py:13
  229.1 6.5 %copy-start.2 = (bf16[2048,512]{1,0:T(8,128)(2,1)S(1)}, bf16[2048,512]{1,0:T(8,128)(2,1)}, u32[]{:S(2)}) copy-start(bf16[2048,512]{1,0:T(8,128)(2,1)} %param.10) | copy-start | bytes 6291460
  235.6 0.7 copy-start.8
  236.3 1.9 copy-start.3
Sparse Core Ops, SparseCore 0:
  16.3 25.2 all-gather.11
  121.3 33.4 all-reduce.1
  157.9 27.9 all-gather.13
  192.8 27.4 all-gather.15
  229.0 27.4 all-gather.17
  263.2 27.4 all-gather.19
